TPU v7x, 256 devices: a whole 4x4x8 slice. The times are simulated.
256 devices in a mesh: rep: 32 (over x, y, core), tp: 8 (over z).
Axes of the slice: x: 4, y: 4, z: 8, core: 2. Of those that a mesh axis runs over, the one named last changes fastest.
Arguments:
- hidden_in: bfloat16 [3072, 8192], P('rep', 'tp'), may hold values from -6 to 6
- queries: bfloat16 [3072, 8192], P('rep', 'tp'), may hold values from -20 to 20
- cache_keys: bfloat16 [3072, 128, 1024], P('rep', None, 'tp'), may hold values from -6 to 6
- cached_value_rows: bfloat16 [3072, 128, 1024], P('rep', None, 'tp'), may hold values from -6 to 6
- cache_lengths: int32 [3072], P('rep'), may hold values from 1 to 128, 98304 in all
- base_key_matrix: bfloat16 [8192, 1024], P(None, 'tp'), may hold values from -0.0625 to 0.0625
- base_value_matrix: bfloat16 [8192, 1024], P(None, 'tp'), may hold values from -0.0625 to 0.0625
- shrink_weights: bfloat16 [128, 8192, 128], P('rep', 'tp'), may hold values from -0.0625 to 0.0625
- pooled_up_weights: bfloat16 [128, 2, 64, 1024], P('rep', None, None, 'tp'), may hold values from -0.75 to 0.75
- block_owner: int32 [768, 1], P('rep'), may hold values from 0 to 31; in each aligned block of 24 rows (0 to 23, 24 to 47, ...) at most 2 rows name the same one
- block_slot: int32 [768], P('rep'), may hold values from 0 to 3
Outputs:
- new_keys: bfloat16 [3072, 1024], P('rep', 'tp')
- new_values: bfloat16 [3072, 1024], P('rep', 'tp')
- context: bfloat16 [3072, 8192], P('rep', 'tp')
Inputs may be any that keep to these rules, and one draw needn't show every extreme that they name: `block_owner`: among the 24 blocks of one replica group at most 2 name the same owner, and some group in every draw has 2 blocks with one owner.
All inputs are finite; a program needn't handle non-finite values. No bound on the sum of `cache_lengths` on one device may be relied on, other than what follows from the above.
Results may differ from a plain program's by a relative error of at most 0.0055.
Values may be sent and summed in bfloat16 or wider, within the bound.
A program may use at most 128 MiB of HBM per device.

v0:
```python
import jax
import jax.numpy as jnp
from jax import lax
from jax.sharding import PartitionSpec as P

HEAD_SIZE = 128
BLK = 4
adapter_scale = 0.5
masked_score = -1e30


def attend(group_queries, key_cache, value_cache, lengths, fresh_keys, fresh_values):
    rows_here = group_queries.shape[0]
    head_groups = key_cache.shape[2] // HEAD_SIZE
    group_size = group_queries.shape[1] // (head_groups * HEAD_SIZE)
    window = key_cache.shape[1]
    inverse_root = HEAD_SIZE ** (-0.5)
    query_heads = group_queries.reshape(rows_here, head_groups, group_size, HEAD_SIZE)
    key_heads = key_cache.reshape(rows_here, window, head_groups, HEAD_SIZE)
    value_heads = value_cache.reshape(rows_here, window, head_groups, HEAD_SIZE)
    scores = (
        jnp.einsum("rkgd,rtkd->rkgt", query_heads, key_heads, preferred_element_type=jnp.float32)
        * inverse_root
    )
    own_score = (
        jnp.einsum(
            "rkgd,rkd->rkg",
            query_heads,
            fresh_keys.reshape(rows_here, head_groups, HEAD_SIZE),
            preferred_element_type=jnp.float32,
        )
        * inverse_root
    )
    visible = (jnp.arange(window, dtype=jnp.int32)[None, :] < lengths[:, None])[:, None, None, :]
    highest = jnp.maximum(jnp.max(jnp.where(visible, scores, masked_score), axis=-1), own_score)
    exp_terms = jnp.where(visible, jnp.exp(scores - highest[..., None]), 0.0)
    own_term = jnp.exp(own_score - highest)
    denominator = jnp.sum(exp_terms, axis=-1) + own_term
    weights = (exp_terms / denominator[..., None]).astype(jnp.bfloat16)
    own_weight = (own_term / denominator).astype(jnp.bfloat16)
    context = jnp.einsum(
        "rkgt,rtkd->rkgd", weights, value_heads, preferred_element_type=jnp.float32
    )
    context = context + own_weight.astype(jnp.float32)[..., None] * fresh_values.reshape(
        rows_here, head_groups, 1, HEAD_SIZE
    ).astype(jnp.float32)
    return context.reshape(rows_here, -1).astype(jnp.bfloat16)


def earlier_ranks(owners):
    span_count = owners.shape[-1]
    matching = owners[..., :, None] == owners[..., None, :]
    before = jnp.arange(span_count)[:, None] > jnp.arange(span_count)[None, :]
    return jnp.sum((matching & before).astype(jnp.int32), axis=-1)


def slot_layout(owners_all, slots_all, myself, replicas, blocks_here, capacity):
    owners_grid = owners_all.reshape(replicas, blocks_here)
    slots_grid = slots_all.reshape(replicas, blocks_here)
    ranks_grid = earlier_ranks(owners_grid)
    placed = (owners_grid == myself)[:, :, None] & (
        ranks_grid[:, :, None] == jnp.arange(capacity, dtype=jnp.int32)[None, None, :]
    )
    placed_int = placed.astype(jnp.int32)
    slot_index = jnp.sum(placed_int * slots_grid[:, :, None], axis=1).reshape(replicas * capacity)
    return (placed, slot_index)


def adapter_pass(slot_rows, slot_index, shrink_weights, pooled_up_weights, site_sum):
    chosen_shrink = jnp.take(shrink_weights, slot_index, axis=0)
    selected_expand = jnp.take(pooled_up_weights, slot_index, axis=0)
    partial_value = jnp.einsum(
        "snd,sdr->snr", slot_rows, chosen_shrink, preferred_element_type=jnp.float32
    )
    shrunk = site_sum(partial_value).astype(jnp.bfloat16)
    split_halves = shrunk.reshape(shrunk.shape[0], shrunk.shape[1], 2, shrunk.shape[2] // 2)
    summed_terms = jnp.einsum(
        "snkr,skrw->snkw", split_halves, selected_expand, preferred_element_type=jnp.float32
    )
    return (adapter_scale * summed_terms).astype(jnp.bfloat16)


def shards(
    hidden_in,
    queries,
    cache_keys,
    cached_value_rows,
    cache_lengths,
    base_key_matrix,
    base_value_matrix,
    shrink_weights,
    pooled_up_weights,
    block_owner,
    block_slot,
):
    rows_here = hidden_in.shape[0]
    shard_width = hidden_in.shape[1]
    replicas = lax.axis_size("rep")
    myself = lax.axis_index("rep")
    blocks_here = rows_here // BLK
    capacity = max(2, (2 * blocks_here + replicas - 1) // replicas)
    key_row_width = base_key_matrix.shape[1]
    gathered = lax.all_gather(hidden_in, "tp", axis=1, tiled=True)
    base_keys = jnp.dot(gathered, base_key_matrix, preferred_element_type=jnp.float32)
    base_values = jnp.dot(gathered, base_value_matrix, preferred_element_type=jnp.float32)
    owners_all, slots_all = (
        lax.all_gather(block_owner[:, 0], "rep", axis=0, tiled=True),
        lax.all_gather(block_slot, "rep", axis=0, tiled=True),
    )
    placed, slot_index = slot_layout(owners_all, slots_all, myself, replicas, blocks_here, capacity)
    every_row = lax.all_gather(hidden_in, "rep", axis=0, tiled=True)
    same_group = jnp.eye(replicas, dtype=jnp.bfloat16)
    compactor = jnp.einsum("pq,qbc->pcqb", same_group, placed.astype(jnp.bfloat16)).reshape(
        replicas * capacity, replicas * blocks_here
    )
    slot_rows = jnp.dot(
        compactor,
        every_row.reshape(replicas * blocks_here, BLK * shard_width),
        preferred_element_type=jnp.float32,
    ).astype(jnp.bfloat16)
    slot_rows = slot_rows.reshape(replicas * capacity, BLK, shard_width)

    def sum_every(partial_value):
        return lax.psum(partial_value, "tp")

    deltas = adapter_pass(slot_rows, slot_index, shrink_weights, pooled_up_weights, sum_every)
    spread = jnp.einsum(
        "sq,sx->qx",
        compactor,
        deltas.reshape(replicas * capacity, BLK * 2 * key_row_width),
        preferred_element_type=jnp.float32,
    )
    spread = spread.reshape(replicas * rows_here, 2, key_row_width)
    per_row_delta = lax.psum_scatter(
        spread.astype(jnp.bfloat16), "rep", scatter_dimension=0, tiled=True
    ).astype(jnp.float32)
    fresh_keys = (base_keys + per_row_delta[:, 0]).astype(jnp.bfloat16)
    fresh_values = (base_values + per_row_delta[:, 1]).astype(jnp.bfloat16)
    context = attend(
        queries, cache_keys, cached_value_rows, cache_lengths, fresh_keys, fresh_values
    )
    return (fresh_keys, fresh_values, context)


def solution(mesh):
    return jax.shard_map(
        shards,
        mesh=mesh,
        in_specs=(
            P("rep", "tp"),
            P("rep", "tp"),
            P("rep", None, "tp"),
            P("rep", None, "tp"),
            P("rep"),
            P(None, "tp"),
            P(None, "tp"),
            P("rep", "tp", None),
            P("rep", None, None, "tp"),
            P("rep", None),
            P("rep"),
        ),
        out_specs=(P("rep", "tp"), P("rep", "tp"), P("rep", "tp")),
        check_vma=False,
    )
```

profile of v0, /device:TPU:2, one launch (start us, length us, event | category | flops | bytes accessed | tf_op | source)
XLA Modules:
  0.0 236.1 jit_solution(2521708871560459143)
XLA Ops:
  8.8 1.4 dynamic-slice
  10.9 0.9 dynamic-update-slice.1
  12.5 15.9 %all-reduce.2 = (s32[768]{0:T(1024)S(1)}, s32[768]{0:T(1024)S(1)}) all-reduce(s32[768]{0:T(1024)S(1)} %bitcast_dynamic-update-slice_fusion, s32[768]{0:T(1024)S(1)} %dynamic-update-slice.1), channel_id=2, replica_groups=mesh['rep'=32,'tp'=8] {'rep'}, use_global_device_ids=true, to_apply=%add | all-reduce | flops 1536 | bytes 12288
  29.3 1.0 multiply_bitcast_fusion
  30.3 1.7 reshape.170
  32.1 2.1 gather_fusion
  34.2 8.6 %gather_fusion.1 = bf16[64,1024,128]{2,1,0:T(8,128)(2,1)} fusion(bf16[4,1024,128]{2,1,0:T(8,128)(2,1)} %param.18, s32[1024]{0:T(1024)S(1)} %pad_clamp_fusion), kind=kCustom, calls=%fused_computation.1 | custom fusion | bytes 33554688 | tf_op jit(solution)/shard_map/jit(_take)/gather | solution.py:70
  42.8 24.6 %all-gather.6.cloned.1.call-done = bf16[3072,1024]{1,0:T(8,128)(2,1)} async-done(((bf16[96,1024]{1,0:T(8,128)(2,1)}), bf16[3072,1024]{1,0:T(8,128)(2,1)}) %all-gather.6.cloned.1.call-update) | async-done | bytes 6291472 | tf_op jit(solution)/shard_map/all_gather | solution.py:111
  67.4 10.7 %reshape.173 = bf16[768,4096]{1,0:T(8,128)(2,1)} reshape(bf16[3072,1024]{1,0:T(8,128)(2,1)} %all-gather.6.cloned.1.call-done) | data formatting | bytes 12582912 | tf_op jit(solution)/shard_map/reshape | solution.py:118
  78.1 4.8 %convolution_convert_fusion = bf16[64,4096]{1,0:T(8,128)(2,1)} fusion(bf16[64,768]{1,0:T(8,128)(2,1)S(1)} %reshape.170, bf16[768,4096]{1,0:T(8,128)(2,1)} %reshape.173), kind=kOutput, calls=%fused_computation.6 | convolution fusion | flops 402915328 | bytes 6914048 | tf_op jit(solution)/shard_map/dot_general | solution.py:116
  82.9 2.2 reshape.174
  85.1 8.7 %fusion = f32[64,4,128]{2,1,0:T(4,128)S(1)} fusion(bf16[64,4,1024]{2,1,0:T(4,128)(2,1)} %reshape.174, bf16[64,1024,128]{2,1,0:T(8,128)(2,1)} %gather_fusion.1, pred[64]{0:T(512)(128)(4,1)S(1)} %compare_and_fusion), kind=kOutput, calls=%fused_computation.2 | convolution fusion | flops 75497472 | bytes 17432640 | tf_op jit(solution)/shard_map/snd,sdr->snr/dot_general | solution.py:72
  93.7 31.5 %all-reduce.4 = bf16[64,4,128]{2,1,0:T(4,128)(2,1)S(1)} all-reduce(f32[64,4,128]{2,1,0:T(4,128)S(1)} %fusion), channel_id=1, replica_groups=mesh['rep'=32,'tp'=8] {'tp'}, use_global_device_ids=true, to_apply=%region_2.3 | all-reduce | flops 32768 | bytes 196608 | tf_op jit(solution)/shard_map/psum | solution.py:124
  125.3 2.3 fusion.14
  127.8 1.7 convolution_convert_fusion.1
  129.6 3.8 %convert_element_type.61 = bf16[3072,2,128]{2,1,0:T(2,128)(2,1)} reshape(bf16[768,1024]{1,0:T(8,128)(2,1)} %convolution_convert_fusion.1) | data formatting | bytes 3145728 | tf_op jit(solution)/shard_map/convert_element_type | solution.py:135
  133.4 2.8 %copy.30 = bf16[3072,2,128]{2,0,1:T(8,128)(2,1)} copy(bf16[3072,2,128]{2,1,0:T(2,128)(2,1)} %convert_element_type.61) | data formatting | bytes 3145728 | tf_op jit(solution)/shard_map/convert_element_type | solution.py:135
  137.5 2.4 %select_reduce_fusion = (f32[96,8]{1,0:T(8,128)}, f32[96,8,128]{2,1,0:T(8,128)S(1)}) fusion(pred[96,128]{1,0:T(8,128)(4,1)S(1)} %iota_compare_fusion, bf16[96,8,128]{2,1,0:T(8,128)(2,1)S(1)} %bitcast.43, bf16[96,128,128]{2,1,0:T(8,128)(2,1)S(1)} %copy-done), kind=kOutput, calls=%fused_computation.25 | convolution fusion | flops 25459968 | bytes 3750912 | tf_op jit(solution)/shard_map/rkgd,rtkd->rkgt/dot_general | solution.py:22
  140.0 79.3 %reduce-scatter.2.cloned.1.call-done = bf16[96,2,128]{2,0,1:T(8,128)(2,1)} async-done(((bf16[3072,2,128]{2,0,1:T(8,128)(2,1)}), bf16[96,2,128]{2,0,1:T(8,128)(2,1)}) %reduce-scatter.2.cloned.1.call-update) | async-done | bytes 49168 | tf_op jit(solution)/shard_map/reduce_scatter | solution.py:134
  219.3 1.4 convert_element_type.62
  220.8 2.8 %fusion.17 = bf16[96,128]{1,0:T(8,128)(2,1)S(1)} fusion(bf16[96,8192]{1,0:T(8,128)(2,1)} %all-gather.4.cloned.1.call-done, bf16[8192,128]{1,0:T(8,128)(2,1)} %param.16, f32[96,2,128]{2,0,1:T(8,128)} %convert_element_type.62), kind=kOutput, calls=%fused_computation.19 | convolution fusion | flops 201351168 | bytes 3743744 | tf_op jit(solution)/shard_map/dot_general | solution.py:104
  223.6 1.2 fusion.26
  225.1 1.2 fusion.38
  227.0 1.0 fusion.7
  (57 shorter events, 5.7 us)
Async XLA Ops:
  8.0 129.6 %copy-start = (bf16[96,128,128]{2,1,0:T(8,128)(2,1)S(1)}, bf16[96,128,128]{2,1,0:T(8,128)(2,1)}, u32[]{:S(2)}) copy-start(bf16[96,128,128]{2,1,0:T(8,128)(2,1)} %param.13) | copy-start | bytes 9437188
  8.0 24.0 %copy-start.1 = (bf16[4,2,64,128]{3,2,1,0:T(8,128)(2,1)S(1)}, bf16[4,2,64,128]{3,2,1,0:T(8,128)(2,1)}, u32[]{:S(2)}) copy-start(bf16[4,2,64,128]{3,2,1,0:T(8,128)(2,1)} %param.19) | copy-start | bytes 393220
  8.0 59.3 %all-gather.6.cloned.1.call-start = ((), (), s32[]{:S(2)}) async-start(), calls=%async_computation.2 | async-start | bytes 6488064 | tf_op jit(solution)/shard_map/all_gather | solution.py:111
  8.8 210.6 %reduce-scatter.2.cloned.1.call-start = ((), (), s32[]{:S(2)}) async-start(), calls=%async_computation.3 | async-start | bytes 1622016 | tf_op jit(solution)/shard_map/reduce_scatter | solution.py:134
  133.4 3.4 %copy-start.7 = (bf16[96,1024]{1,0:T(8,128)(2,1)S(1)}, bf16[96,1024]{1,0:T(8,128)(2,1)}, u32[]{:S(2)}) copy-start(bf16[96,1024]{1,0:T(8,128)(2,1)} %param.12) | copy-start | bytes 589828
  133.4 3.5 %copy-start.9 = (s32[96]{0:T(128)S(1)}, s32[96]{0:T(128)}, u32[]{:S(2)}) copy-start(s32[96]{0:T(128)} %param.15) | copy-start | bytes 1156
  136.2 84.5 %all-gather.4.cloned.1.call-start = ((), (), s32[]{:S(2)}) async-start(), calls=%async_computation.1 | async-start | bytes 1769472 | tf_op jit(solution)/shard_map/all_gather | solution.py:103
  136.9 0.7 copy-start.4
  220.8 4.0 %copy-start.5 = (f32[96,8]{1,0:T(8,128)S(1)}, f32[96,8]{1,0:T(8,128)}, u32[]{:S(2)}) copy-start(f32[96,8]{1,0:T(8,128)} %get-tuple-element.9) | copy-start | bytes 9220
  220.8 4.4 %copy-start.2 = (bf16[96,8192]{1,0:T(8,128)(2,1)S(1)}, bf16[96,8192]{1,0:T(8,128)(2,1)}, u32[]{:S(2)}) copy-start(bf16[96,8192]{1,0:T(8,128)(2,1)} %all-gather.4.cloned.1.call-done) | copy-start | bytes 4718596
  220.8 4.4 %copy-start.3 = (bf16[8192,128]{1,0:T(8,128)(2,1)S(1)}, bf16[8192,128]{1,0:T(8,128)(2,1)}, u32[]{:S(2)}) copy-start(bf16[8192,128]{1,0:T(8,128)(2,1)} %param.17) | copy-start | bytes 6291460
  220.8 4.4 %copy-start.6 = (f32[96,2,128]{2,0,1:T(8,128)S(1)}, f32[96,2,128]{2,0,1:T(8,128)}, u32[]{:S(2)}) copy-start(f32[96,2,128]{2,0,1:T(8,128)} %convert_element_type.62) | copy-start | bytes 294916
  223.5 2.8 %copy-start.8 = (bf16[96,128]{1,0:T(8,128)(2,1)}, bf16[96,128]{1,0:T(8,128)(2,1)S(1)}, u32[]{:S(2)}) copy-start(bf16[96,128]{1,0:T(8,128)(2,1)S(1)} %fusion.17) | copy-start | bytes 73732
  225.1 1.9 copy-start.10
Sparse Core Ops, SparseCore 0:
  11.4 55.9 all-gather.5
  136.3 82.9 reduce-scatter.1
Sparse Core Ops, SparseCore 1:
  138.5 36.9 all-gather.3
where the time goes:
time: 237 us; the launch traced here: 236 us
  waiting for transfers between devices  105 us (44%)
  blocking collectives  47.3 us (20%)
  local copies, waits for them, and re-layouts  37.9 us (16%)
  matrix products  26 us (11%)
  between operations  16.4 us (7%)
  other arithmetic  3.18 us (1%)
    reduce_scatter x1, waiting for transfers between devices, shards(): lax.psum_scatter(spread.astype(jnp.bfloat16), 'rep', scatter_dimension=0,...  79.3 us
    psum x1, blocking collectives, sum_every(): return lax.psum(partial_value, 'tp')  31.5 us
    all_gather x1, waiting for transfers between devices, shards(): every_row = lax.all_gather(hidden_in, 'rep', axis=0, tiled=True)  24.6 us
    unnamed x1, blocking collectives  15.9 us
    reshape x1, local copies, waits for them, and re-layouts, shards(): every_row.reshape(replicas * blocks_here, BLK * shard_width)  10.7 us
    dot_general x1, matrix products, adapter_pass(): jnp.einsum('snd,sdr->snr', slot_rows, chosen_shrink, preferred_element_ty...  8.66 us
    gather x1, local copies, waits for them, and re-layouts, adapter_pass(): chosen_shrink = jnp.take(shrink_weights, slot_index, axis=0)  8.6 us
    convert_element_type x2, local copies, waits for them, and re-layouts, shards(): spread.astype(jnp.bfloat16)  6.61 us
  transfers between devices with their start and end apart: 3, of which 2 were waited for; matrix products, arithmetic and copies ran while one was open for 9% of the time, Pallas kernels for 0%

commit v1 on v0

--- a/solution.py
+++ b/solution.py
@@ -121,7 +121,7 @@
     slot_rows = slot_rows.reshape(replicas * capacity, BLK, shard_width)
 
     def sum_every(partial_value):
-        return lax.psum(partial_value, "tp")
+        return jnp.sum(lax.all_gather(partial_value, "tp"), axis=0)
 
     deltas = adapter_pass(slot_rows, slot_index, shrink_weights, pooled_up_weights, sum_every)
     spread = jnp.einsum(

time: 237 us -> 285 us (1.20)
  waiting for transfers between devices: 105 us -> 184 us
  blocking collectives: 47.3 us -> 15.9 us
    all_gather x1, waiting for transfers between devices: 0.01 us -> 39.5 us  [shards(): gathered = lax.all_gather(hidden_in, 'tp', axis=1, tiled=True)]
    all_gather x0 -> x1, waiting for transfers between devices: none -> 36.2 us  [sum_every(): return jnp.sum(lax.all_gather(partial_value, 'tp'), axis=0)]
    psum x1 -> x0, blocking collectives: 31.5 us -> none  [sum_every(): return lax.psum(partial_value, 'tp')]
  transfers between devices with their start and end apart: 3 -> 4, of which waited for: 2 -> 4; matrix products, arithmetic and copies ran while one was open for 9% -> 8% of each run, Pallas kernels for 0% -> 0%
where the time goes in v1:
time: 285 us; the launch traced here: 284 us
  waiting for transfers between devices  184 us (65%)
  local copies, waits for them, and re-layouts  38 us (13%)
  matrix products  26.8 us (9%)
  blocking collectives  15.9 us (6%)
  between operations  14.7 us (5%)
  other arithmetic  4.61 us (2%)
    reduce_scatter x1, waiting for transfers between devices, shards(): lax.psum_scatter(spread.astype(jnp.bfloat16), 'rep', scatter_dimension=0,...  80.5 us
    all_gather x1, waiting for transfers between devices, shards(): gathered = lax.all_gather(hidden_in, 'tp', axis=1, tiled=True)  39.5 us
    all_gather x1, waiting for transfers between devices, sum_every(): return jnp.sum(lax.all_gather(partial_value, 'tp'), axis=0)  36.2 us
    all_gather x1, waiting for transfers between devices, shards(): every_row = lax.all_gather(hidden_in, 'rep', axis=0, tiled=True)  26.7 us
    unnamed x1, blocking collectives  15.9 us
    reshape x1, local copies, waits for them, and re-layouts, shards(): every_row.reshape(replicas * blocks_here, BLK * shard_width)  10.7 us
    dot_general x1, matrix products, adapter_pass(): jnp.einsum('snd,sdr->snr', slot_rows, chosen_shrink, preferred_element_ty...  9.36 us
    gather x1, local copies, waits for them, and re-layouts, adapter_pass(): chosen_shrink = jnp.take(shrink_weights, slot_index, axis=0)  8.64 us
  transfers between devices with their start and end apart: 4, of which 4 were waited for; matrix products, arithmetic and copies ran while one was open for 8% of the time, Pallas kernels for 0%

profile of v1, /device:TPU:2, one launch (start us, length us, event | category | flops | bytes accessed | tf_op | source)
XLA Modules:
  0.0 284.2 jit_solution(15611733196950218567)
XLA Ops:
  8.0 1.4 dynamic-slice
  11.6 15.9 %all-reduce.2 = (s32[768]{0:T(1024)S(1)}, s32[768]{0:T(1024)S(1)}) all-reduce(s32[768]{0:T(1024)S(1)} %bitcast_dynamic-update-slice_fusion, s32[768]{0:T(1024)S(1)} %dynamic-update-slice.1), channel_id=2, replica_groups=mesh['rep'=32,'tp'=8] {'rep'}, use_global_device_ids=true, to_apply=%add | all-reduce | flops 1536 | bytes 12288
  29.5 1.7 reshape.170
  31.2 8.6 %gather_fusion.1 = bf16[64,1024,128]{2,1,0:T(8,128)(2,1)} fusion(bf16[4,1024,128]{2,1,0:T(8,128)(2,1)} %param.18, s32[1024]{0:T(1024)S(1)} %pad_clamp_fusion), kind=kCustom, calls=%fused_computation.1 | custom fusion | bytes 33554688 | tf_op jit(solution)/shard_map/jit(_take)/gather | solution.py:70
  39.8 26.7 %all-gather.8.cloned.1.call-done = bf16[3072,1024]{1,0:T(8,128)(2,1)} async-done(((bf16[96,1024]{1,0:T(8,128)(2,1)}), bf16[3072,1024]{1,0:T(8,128)(2,1)}) %all-gather.8.cloned.1.call-update) | async-done | bytes 6291472 | tf_op jit(solution)/shard_map/all_gather | solution.py:111
  66.5 10.7 %reshape.173 = bf16[768,4096]{1,0:T(8,128)(2,1)} reshape(bf16[3072,1024]{1,0:T(8,128)(2,1)} %all-gather.8.cloned.1.call-done) | data formatting | bytes 12582912 | tf_op jit(solution)/shard_map/reshape | solution.py:118
  77.3 4.8 %convolution_convert_fusion = bf16[64,4096]{1,0:T(8,128)(2,1)} fusion(bf16[64,768]{1,0:T(8,128)(2,1)S(1)} %reshape.170, bf16[768,4096]{1,0:T(8,128)(2,1)} %reshape.173), kind=kOutput, calls=%fused_computation.6 | convolution fusion | flops 402915328 | bytes 6914048 | tf_op jit(solution)/shard_map/dot_general | solution.py:116
  82.0 2.2 reshape.174
  84.3 9.4 %fusion = f32[64,4,128]{2,1,0:T(4,128)} fusion(bf16[64,4,1024]{2,1,0:T(4,128)(2,1)} %reshape.174, bf16[64,1024,128]{2,1,0:T(8,128)(2,1)} %gather_fusion.1, pred[64]{0:T(512)(128)(4,1)S(1)} %compare_and_fusion), kind=kOutput, calls=%fused_computation.2 | convolution fusion | flops 75497472 | bytes 17432640 | tf_op jit(solution)/shard_map/snd,sdr->snr/dot_general | solution.py:72
  93.7 2.2 gather_fusion
  95.9 36.2 %all-gather.10.cloned.1.call-done = f32[512,4,128]{2,1,0:T(4,128)} async-done(((f32[64,4,128]{2,1,0:T(4,128)}), f32[512,4,128]{2,1,0:T(4,128)}) %all-gather.10.cloned.1.call-update) | async-done | bytes 1048592 | tf_op jit(solution)/shard_map/all_gather | solution.py:124
  132.1 1.4 reduce_sum.38
  133.6 2.3 fusion.14
  136.1 1.8 convolution_convert_fusion.1
  137.9 3.8 %convert_element_type.66 = bf16[3072,2,128]{2,1,0:T(2,128)(2,1)} reshape(bf16[768,1024]{1,0:T(8,128)(2,1)} %convolution_convert_fusion.1) | data formatting | bytes 3145728 | tf_op jit(solution)/shard_map/convert_element_type | solution.py:135
  141.7 2.8 copy.31
  145.8 2.4 select_reduce_fusion
  148.2 80.5 %reduce-scatter.2.cloned.1.call-done = bf16[96,2,128]{2,0,1:T(8,128)(2,1)} async-done(((bf16[3072,2,128]{2,0,1:T(8,128)(2,1)}), bf16[96,2,128]{2,0,1:T(8,128)(2,1)}) %reduce-scatter.2.cloned.1.call-update) | async-done | bytes 49168 | tf_op jit(solution)/shard_map/reduce_scatter | solution.py:134
  228.8 1.5 convert_element_type.67
  230.2 39.5 %all-gather.6.cloned.1.call-done = bf16[96,8192]{1,0:T(8,128)(2,1)} async-done(((bf16[96,1024]{1,0:T(8,128)(2,1)}), bf16[96,8192]{1,0:T(8,128)(2,1)}) %all-gather.6.cloned.1.call-update) | async-done | bytes 1572880 | tf_op jit(solution)/shard_map/all_gather | solution.py:103
  269.8 2.8 fusion.17
  272.6 1.2 fusion.26
  274.1 1.2 fusion.38
  276.0 1.0 fusion.7
  (60 shorter events, 7.6 us)
Async XLA Ops:
  7.2 138.7 %copy-start = (bf16[96,128,128]{2,1,0:T(8,128)(2,1)S(1)}, bf16[96,128,128]{2,1,0:T(8,128)(2,1)}, u32[]{:S(2)}) copy-start(bf16[96,128,128]{2,1,0:T(8,128)(2,1)} %param.13) | copy-start | bytes 9437188
  7.2 59.3 %all-gather.8.cloned.1.call-start = ((), (), s32[]{:S(2)}) async-start(), calls=%async_computation.2 | async-start | bytes 6488064 | tf_op jit(solution)/shard_map/all_gather | solution.py:111
  7.9 124.2 %all-gather.10.cloned.1.call-start = ((), (), s32[]{:S(2)}) async-start(), calls=%async_computation.4 | async-start | bytes 1179648 | tf_op jit(solution)/shard_map/all_gather | solution.py:124
  84.3 9.4 %copy-start.1 = (bf16[4,2,64,128]{3,2,1,0:T(8,128)(2,1)S(1)}, bf16[4,2,64,128]{3,2,1,0:T(8,128)(2,1)}, u32[]{:S(2)}) copy-start(bf16[4,2,64,128]{3,2,1,0:T(8,128)(2,1)} %param.19) | copy-start | bytes 393220
  93.7 135.1 %reduce-scatter.2.cloned.1.call-start = ((), (), s32[]{:S(2)}) async-start(), calls=%async_computation.3 | async-start | bytes 1622016 | tf_op jit(solution)/shard_map/reduce_scatter | solution.py:134
  141.7 3.4 %copy-start.7 = (bf16[96,1024]{1,0:T(8,128)(2,1)S(1)}, bf16[96,1024]{1,0:T(8,128)(2,1)}, u32[]{:S(2)}) copy-start(bf16[96,1024]{1,0:T(8,128)(2,1)} %param.12) | copy-start | bytes 589828
  141.7 3.5 %copy-start.9 = (s32[96]{0:T(128)S(1)}, s32[96]{0:T(128)}, u32[]{:S(2)}) copy-start(s32[96]{0:T(128)} %param.15) | copy-start | bytes 1156
  144.5 125.3 %all-gather.6.cloned.1.call-start = ((), (), s32[]{:S(2)}) async-start(), calls=%async_computation.1 | async-start | bytes 1769472 | tf_op jit(solution)/shard_map/all_gather | solution.py:103
  145.1 0.7 copy-start.4
  269.8 4.0 %copy-start.5 = (f32[96,8]{1,0:T(8,128)S(1)}, f32[96,8]{1,0:T(8,128)}, u32[]{:S(2)}) copy-start(f32[96,8]{1,0:T(8,128)} %get-tuple-element.9) | copy-start | bytes 9220
  269.8 4.3 %copy-start.2 = (bf16[96,8192]{1,0:T(8,128)(2,1)S(1)}, bf16[96,8192]{1,0:T(8,128)(2,1)}, u32[]{:S(2)}) copy-start(bf16[96,8192]{1,0:T(8,128)(2,1)} %all-gather.6.cloned.1.call-done) | copy-start | bytes 4718596
  269.8 4.4 %copy-start.3 = (bf16[8192,128]{1,0:T(8,128)(2,1)S(1)}, bf16[8192,128]{1,0:T(8,128)(2,1)}, u32[]{:S(2)}) copy-start(bf16[8192,128]{1,0:T(8,128)(2,1)} %param.17) | copy-start | bytes 6291460
  269.8 4.4 %copy-start.6 = (f32[96,2,128]{2,0,1:T(8,128)S(1)}, f32[96,2,128]{2,0,1:T(8,128)}, u32[]{:S(2)}) copy-start(f32[96,2,128]{2,0,1:T(8,128)} %convert_element_type.67) | copy-start | bytes 294916
  272.5 2.8 copy-start.8
  274.1 1.9 copy-start.10
Sparse Core Ops, SparseCore 0:
  10.5 55.9 all-gather.7
  93.8 38.2 all-gather.9
  144.6 84.1 reduce-scatter.1
  230.4 39.2 all-gather.5
